TPU v7x, 32 devices: a whole 2x2x4 slice. The times are simulated.
32 devices in a mesh: groups: 2 (over y), seq: 4 (over z), section: 2 (over x), kv: 2 (over core).
Axes of the slice: x: 2, y: 2, z: 4, core: 2. Of those that a mesh axis runs over, the one named last changes fastest.
Arguments:
- queries: bfloat16 [4, 1024, 2560], P(('groups', 'section'), 'seq', 'kv'), parts along dimension 0, may hold values from -128 to 128
- key_rows: bfloat16 [4, 1024, 512], P(('groups', 'section'), 'seq', 'kv'), parts along dimension 0, may hold values from -4 to 4
- values: bfloat16 [4, 1024, 512], P(('groups', 'section'), 'seq', 'kv'), parts along dimension 0, may hold values from -6 to 6
- lengths: int32 [4, 3], P(('groups', 'section')), parts along dimension 0, may hold values from 1 to 32, 64 in all within a row
- block_order: int32 [4, 4], P(('groups', 'section')), parts along dimension 0, may hold values from 0 to 3, each once within a row
- page_owner: int32 [4, 64, 1], P(('groups', 'section')), parts along dimension 0, may hold values from 0 to 3; in each aligned block of 16 rows (0 to 15, 16 to 31, ..., all dimensions but the last counted through in order) at most 8 rows name the same one
Outputs:
- handed: bfloat16 [4, 1024, 2560], P(('groups', 'section'), 'seq', 'kv'), parts along dimension 0
- cache_keys: bfloat16 [4, 4, 512, 512], P(('groups', 'section'), 'seq', None, 'kv'), parts along dimension 0
- cache_values: bfloat16 [4, 4, 512, 512], P(('groups', 'section'), 'seq', None, 'kv'), parts along dimension 0
There are 2 independent parts, one for each index of `groups`. A program takes and returns all parts, laid end to end along the dimension named above; each array names one. Nothing has to cross between parts.
Inputs may be any that keep to these rules, and one draw needn't show every extreme that they name: `lengths`: lengths sum to 64; the longest request has exactly 32 pages. `block_order`: each row is a permutation of the seq indices. `page_owner`: among the 16 pages of one aligned device block, no owner is named more than 8 times.
All inputs are finite; a program needn't handle non-finite values.
Results may differ from a plain program's by a relative error of at most 0.0038.
Values may be sent and summed in bfloat16 or wider, within the bound.
No kernel may reach another device: no remote copies, remote signals or barrier semaphores. Data moves between devices by JAX's collectives and lax.ppermute only.
A program may use at most 64 MiB of HBM per device.

v0:
```python
import math

import jax
import jax.numpy as jnp
from jax import lax
from jax.experimental import pallas as pl
from jax.experimental.pallas import tpu as pltpu
from jax.sharding import PartitionSpec as P


HEAD_SIZE = 128
MASKED = -1e30
SLOTS = 2
EXP2_SCALE = math.log2(math.e) / math.sqrt(HEAD_SIZE)


SMEM = pl.BlockSpec(memory_space=pltpu.SMEM)
VMEM = pl.BlockSpec(memory_space=pltpu.VMEM)
ANY = pl.BlockSpec(memory_space=pl.ANY)


def partner(index, turn, count):
    if count & (count - 1) == 0:
        return index ^ turn
    return (index + turn) % count


def partner_of(index, turn, count):
    if count & (count - 1) == 0:
        return jnp.bitwise_xor(index, turn)
    return lax.rem(index + turn, count)


def source_of(index, turn, count):
    if count & (count - 1) == 0:
        return jnp.bitwise_xor(index, turn)
    return lax.rem(index - turn + count, count)


def split_heads_kernel(keys_ref, values_ref, *message_refs):
    rows = keys_ref.shape[1]
    for head, message_ref in enumerate(message_refs):
        columns = pl.ds(head * HEAD_SIZE, HEAD_SIZE)
        message_ref[:rows, :] = keys_ref[0, :, columns]
        message_ref[rows:, :] = values_ref[0, :, columns]


def split_heads(key_rows, values):
    rows, width = key_rows.shape[1:]
    message = jax.ShapeDtypeStruct((2 * rows, HEAD_SIZE), key_rows.dtype)
    return pl.pallas_call(
        split_heads_kernel,
        out_shape=[message] * (width // HEAD_SIZE),
        in_specs=[VMEM] * 2,
        out_specs=[VMEM] * (width // HEAD_SIZE),
        name="split_heads",
    )(key_rows, values)


def stage_kernel(*refs):
    refs[-1][...] = jnp.zeros_like(refs[-1])


def stage(plan, *arrays):
    return pl.pallas_call(
        stage_kernel,
        out_shape=jax.ShapeDtypeStruct((8, HEAD_SIZE), jnp.float32),
        in_specs=[SMEM] + [ANY] * len(arrays),
        out_specs=VMEM,
        compiler_params=pltpu.CompilerParams(vmem_limit_bytes=2**20),
        name="stage",
    )(plan, *arrays)


def exchange(parts):
    count = lax.axis_size("seq")
    received = []
    for turn in range(1, count):
        route = [(i, partner(i, turn, count)) for i in range(count)]
        received.append(lax.ppermute(parts[turn - 1], "seq", route))
    return received


def gather_turns(message):
    return [message] + exchange([message] * (lax.axis_size("seq") - 1))


def attend_kernel(plan_ref, queries_ref, *refs, count, column, page_tokens):
    block_refs = refs[:count]
    context_ref = refs[count + 1]
    query_ref, held_ref, bias_ref, score_ref, max_ref, sum_ref, acc_ref, sems = refs[count + 2 :]
    rows, width = query_ref.shape
    heads = width // HEAD_SIZE
    pages = rows // page_tokens
    own = lax.axis_index("seq")
    requests = plan_ref.shape[1] - count
    own_block = plan_ref[0, requests + own]

    first_start = jnp.int32(0)
    start = jnp.int32(0)
    starts = []
    for request in range(requests):
        starts.append(start)
        first_start = jnp.where(own_block * pages >= start, start, first_start)
        start = start + plan_ref[0, request]

    def needed(turn):
        block = plan_ref[0, requests + source_of(own, turn, count)]
        return block, (block < own_block) & ((block + 1) * pages > first_start)

    query_copy = pltpu.make_async_copy(
        queries_ref.at[0, :, pl.ds(column, width)], query_ref, sems.at[count]
    )
    copies = [
        pltpu.make_async_copy(block_refs[turn], held_ref.at[turn], sems.at[turn])
        for turn in range(count)
    ]
    copies[0].start()
    query_copy.start()
    for turn in range(1, count):
        pl.when(needed(turn)[1])(copies[turn].start)

    row_page = own_block * pages + lax.broadcasted_iota(jnp.int32, (rows, 1), 0) // page_tokens
    row_start = jnp.zeros((rows, 1), jnp.int32)
    for start in starts:
        row_start = jnp.where(row_page >= start, start, row_start)
    row_start = row_start * page_tokens
    row = lax.broadcasted_iota(jnp.int32, (rows, rows), 0)
    key = lax.broadcasted_iota(jnp.int32, (rows, rows), 1)

    def score(turn, head, before):
        scores = (
            lax.dot_general(
                query_ref[:, head * HEAD_SIZE : (head + 1) * HEAD_SIZE],
                held_ref[turn, :rows, :],
                (((1,), (1,)), ((), ())),
                preferred_element_type=jnp.float32,
            )
            + bias_ref[...]
        )
        score_ref[head % SLOTS] = scores
        top = jnp.broadcast_to(jnp.max(scores, axis=1, keepdims=True), (rows, HEAD_SIZE))
        return top if before is None else jnp.maximum(before, top)

    def weigh(turn, head, top):
        total = jnp.zeros((rows, HEAD_SIZE), jnp.float32)
        pieces = []
        for piece in range(rows // HEAD_SIZE):
            scores = score_ref[head % SLOTS, :, piece * HEAD_SIZE : (piece + 1) * HEAD_SIZE]
            weight = jnp.exp2((scores - top) * EXP2_SCALE)
            total = total + weight
            pieces.append(weight.astype(jnp.bfloat16))
        weights = jnp.concatenate(pieces, axis=1)
        return total, jnp.dot(
            weights, held_ref[turn, rows:, :], preferred_element_type=jnp.float32
        )

    def first_block(head, top):
        total, mixed = weigh(0, head, top)
        max_ref[head] = top
        sum_ref[head] = total
        acc_ref[head] = mixed

    def later_block(turn, head, top):
        total, mixed = weigh(turn, head, top)
        rescale = jnp.exp2((max_ref[head] - top) * EXP2_SCALE)
        max_ref[head] = top
        sum_ref[head] = sum_ref[head] * rescale + total
        acc_ref[head] = acc_ref[head] * rescale + mixed

    allowed = (key >= row_start - own_block * rows) & (key <= row)
    bias_ref[...] = jnp.where(allowed, 0.0, MASKED)
    copies[0].wait()
    query_copy.wait()
    tops = [score(0, 0, None)]
    for head in range(heads):
        if head + 1 < heads:
            tops.append(score(0, head + 1, None))
        first_block(head, tops[head])

    for turn in range(1, count):
        block, wanted = needed(turn)

        @pl.when(wanted)
        def _():
            bias_ref[...] = jnp.where(key >= row_start - block * rows, 0.0, MASKED)
            copies[turn].wait()
            tops = [score(turn, 0, max_ref[0])]
            for head in range(heads):
                if head + 1 < heads:
                    tops.append(score(turn, head + 1, max_ref[head + 1]))
                later_block(turn, head, tops[head])

    for head in range(heads):
        total = jnp.sum(sum_ref[head], axis=1, keepdims=True)
        context_ref[0, :, head * HEAD_SIZE : (head + 1) * HEAD_SIZE] = (
            acc_ref[head] * (1.0 / total)
        ).astype(context_ref.dtype)


def attend(plan, queries, blocks, staged, first, group, page_tokens):
    rows = queries.shape[1]
    count = len(blocks)
    width = group * HEAD_SIZE
    pairs = group * rows * rows * (count + 1) // 2

    def kernel(*refs):
        attend_kernel(
            *refs, count=count, column=first * HEAD_SIZE, page_tokens=page_tokens
        )

    return pl.pallas_call(
        kernel,
        out_shape=jax.ShapeDtypeStruct((1, rows, width), queries.dtype),
        in_specs=[SMEM] + [ANY] * (count + 2),
        out_specs=VMEM,
        scratch_shapes=[
            pltpu.VMEM((rows, width), queries.dtype),
            pltpu.VMEM((count, 2 * rows, HEAD_SIZE), queries.dtype),
            pltpu.VMEM((rows, rows), jnp.float32),
            pltpu.VMEM((SLOTS, rows, rows), jnp.float32),
            pltpu.VMEM((group, rows, HEAD_SIZE), jnp.float32),
            pltpu.VMEM((group, rows, HEAD_SIZE), jnp.float32),
            pltpu.VMEM((group, rows, HEAD_SIZE), jnp.float32),
            pltpu.SemaphoreType.DMA((count + 1,)),
        ],
        compiler_params=pltpu.CompilerParams(vmem_limit_bytes=16 * 2**20),
        cost_estimate=pl.CostEstimate(
            flops=4 * pairs * HEAD_SIZE,
            bytes_accessed=2 * 2 * rows * width + count * 4 * rows * HEAD_SIZE,
            transcendentals=pairs,
        ),
        name="attend",
    )(plan, queries, *blocks, staged)


def for_owner(order_ref, owner_ref, source, owner, pages, act):
    block = order_ref[0, source]

    def page_step(page, rank):
        wanted = owner_ref[block * pages + page] == owner
        pl.when(wanted)(lambda: act(page, rank))
        return rank + wanted.astype(jnp.int32)

    lax.fori_loop(0, pages, page_step, jnp.int32(0))


def page_rows(page, page_tokens, base=0):
    return pl.ds(pl.multiple_of(base + page * page_tokens, page_tokens), page_tokens)


def pack_kernel(order_ref, owner_ref, message_ref, *part_refs, page_tokens):
    count = len(part_refs) + 1
    rows = message_ref.shape[0] // 2
    half = part_refs[0].shape[0] // 2
    own = lax.axis_index("seq")
    for turn in range(1, count):
        part_ref = part_refs[turn - 1]
        part_ref[...] = jnp.zeros_like(part_ref)

        def act(page, rank):
            for base, part_base in ((0, 0), (rows, half)):
                part_ref[page_rows(rank, page_tokens, part_base), :] = message_ref[
                    page_rows(page, page_tokens, base), :
                ]

        owner = partner_of(own, turn, count)
        for_owner(order_ref, owner_ref, own, owner, rows // page_tokens, act)


def pack_pages(block_order, owners, message, slots, page_tokens):
    count = block_order.shape[1]
    part = jax.ShapeDtypeStruct((2 * slots * page_tokens, HEAD_SIZE), message.dtype)

    def kernel(*refs):
        pack_kernel(*refs, page_tokens=page_tokens)

    return pl.pallas_call(
        kernel,
        out_shape=[part] * (count - 1),
        in_specs=[SMEM, SMEM, VMEM],
        out_specs=[VMEM] * (count - 1),
        name="pack_pages",
    )(block_order, owners, message)


def scatter_kernel(order_ref, owner_ref, *refs, columns, page_tokens, slots):
    keys_ref, values_ref = refs[-2:]
    keys_ref[...] = jnp.zeros_like(keys_ref)
    values_ref[...] = jnp.zeros_like(values_ref)
    own = lax.axis_index("seq")
    count = order_ref.shape[1]
    for block_ref, (head, turn) in zip(refs[:-2], columns):
        rows = block_ref.shape[0] // 2
        source = source_of(own, turn, count)
        lanes = pl.ds(head * HEAD_SIZE, HEAD_SIZE)

        def act(page, rank):
            put = page_rows(source * slots + rank, page_tokens)
            keys_ref[0, 0, put, lanes] = block_ref[page_rows(page, page_tokens), :]
            values_ref[0, 0, put, lanes] = block_ref[page_rows(page, page_tokens, rows), :]

        for_owner(order_ref, owner_ref, source, own, rows // page_tokens, act)


def scatter_pages(block_order, owners, blocks, columns, width, page_tokens, slots):
    count = block_order.shape[1]
    cache = jax.ShapeDtypeStruct((1, 1, count * slots * page_tokens, width), blocks[0].dtype)

    def kernel(*refs):
        scatter_kernel(*refs, columns=columns, page_tokens=page_tokens, slots=slots)

    return pl.pallas_call(
        kernel,
        out_shape=[cache, cache],
        in_specs=[SMEM, SMEM] + [VMEM] * len(blocks),
        out_specs=[VMEM, VMEM],
        name="scatter_pages",
    )(block_order, owners, *blocks)


def land_kernel(keys_in_ref, values_in_ref, *refs, head):
    keys_ref, values_ref, sems = refs[-3:]
    part_refs = refs[:-3]
    count = len(part_refs) + 1
    half = part_refs[0].shape[0] // 2
    own = lax.axis_index("seq")
    lanes = pl.ds(head * HEAD_SIZE, HEAD_SIZE)
    copies = []
    for turn in range(1, count):
        source = source_of(own, turn, count)
        put = pl.ds(pl.multiple_of(source * half, half), half)
        for side, cache_ref in enumerate((keys_ref, values_ref)):
            copies.append(
                pltpu.make_async_copy(
                    part_refs[turn - 1].at[pl.ds(side * half, half), :],
                    cache_ref.at[0, 0, put, lanes],
                    sems.at[2 * (turn - 1) + side],
                )
            )
    for copy in copies:
        copy.start()
    for copy in copies:
        copy.wait()


def land_pages(cache_keys, cache_values, parts, head):
    def kernel(*refs):
        land_kernel(*refs, head=head)

    return pl.pallas_call(
        kernel,
        out_shape=[
            jax.ShapeDtypeStruct(cache.shape, cache.dtype) for cache in (cache_keys, cache_values)
        ],
        in_specs=[ANY] * (2 + len(parts)),
        out_specs=[ANY, ANY],
        scratch_shapes=[pltpu.SemaphoreType.DMA((2 * len(parts),))],
        input_output_aliases={0: 0, 1: 1},
        compiler_params=pltpu.CompilerParams(vmem_limit_bytes=48 * 2**20),
        name="land_pages",
    )(cache_keys, cache_values, *parts)


def body(queries, key_rows, values, lengths, block_order, page_owner):
    count = lax.axis_size("seq")
    sections = lax.axis_size("section")
    rows = key_rows.shape[1]
    width = key_rows.shape[2]
    kv_heads = width // HEAD_SIZE
    group = queries.shape[2] // width
    kept = kv_heads - kv_heads // 2
    device_pages = page_owner.shape[1] // count
    page_tokens = rows // device_pages
    slots = max(2, 2 * device_pages // count)
    owners = page_owner.reshape(page_owner.shape[1])
    onward = [(i, (i + 1) % sections) for i in range(sections)]

    def hand_on(array):
        return lax.ppermute(array, "section", onward)

    messages = split_heads(key_rows, values)
    plan = jnp.concatenate([lengths, block_order], axis=1)
    gathered = [gather_turns(messages[head]) for head in range(kept)]
    swapped = [hand_on(messages[head]) for head in range(kept, kv_heads)]
    other_plan = hand_on(plan)
    other_queries = [
        hand_on(queries[:, :, head * group * HEAD_SIZE : (head + 1) * group * HEAD_SIZE])
        for head in range(kept, kv_heads)
    ]
    gathered += [gather_turns(message) for message in swapped]
    parts = []
    for head in range(kept, kv_heads):
        packed = pack_pages(block_order, owners, messages[head], slots, page_tokens)
        parts.append(exchange(packed))
    staged = stage(plan, queries, *messages[:kept])
    handed = []
    for head in range(kept):
        context = attend(plan, queries, gathered[head], staged, head * group, group, page_tokens)
        handed.append(hand_on(context))
    for index, head in enumerate(range(kept, kv_heads)):
        handed.append(
            attend(other_plan, other_queries[index], gathered[head], staged, 0, group, page_tokens)
        )
    columns = [(head, turn) for head in range(kept) for turn in range(count)]
    columns += [(head, 0) for head in range(kept, kv_heads)]
    blocks = [gathered[head][turn] if head < kept else messages[head] for head, turn in columns]
    cache = scatter_pages(block_order, owners, blocks, columns, width, page_tokens, slots)
    for index, head in enumerate(range(kept, kv_heads)):
        cache = land_pages(*cache, parts[index], head)
    return (jnp.concatenate(handed, axis=2), *cache)


def solution(mesh):
    in_specs = (
        P(("groups", "section"), "seq", "kv"),
        P(("groups", "section"), "seq", "kv"),
        P(("groups", "section"), "seq", "kv"),
        P(("groups", "section"), None),
        P(("groups", "section"), None),
        P(("groups", "section"), None, None),
    )
    out_specs = (
        P(("groups", "section"), "seq", "kv"),
        P(("groups", "section"), "seq", None, "kv"),
        P(("groups", "section"), "seq", None, "kv"),
    )
    return jax.shard_map(body, mesh=mesh, in_specs=in_specs, out_specs=out_specs, check_vma=False)
```

profile of v0, /device:TPU:0, one launch (start us, length us, event | category | flops | bytes accessed | tf_op | source)
XLA Modules:
  0.0 54.5 jit_solution(16577844955857594158)
XLA Ops:
  0.6 0.0 copy-start
  0.6 0.0 copy-start.6
  0.7 1.8 %split_heads.1 = (bf16[512,128]{1,0:T(8,128)(2,1)}, bf16[512,128]{1,0:T(8,128)(2,1)}) custom-call(bf16[1,256,256]{2,1,0:T(8,128)(2,1)} %keys_ref.1, bf16[1,256,256]{2,1,0:T(8,128)(2,1)} %values_ref.1), custom_call_target="tpu_custom_call" | custom-call | tf_op jit(solution)/shard_map/split_heads/pallas_call | solution.py:51
  2.4 3.1 %collective-permute-start = (bf16[512,128]{1,0:T(8,128)(2,1)}, bf16[512,128]{1,0:T(8,128)(2,1)S(1)}, u32[]{:S(2)}, u32[]{:S(2)}) collective-permute-start(bf16[512,128]{1,0:T(8,128)(2,1)} %get-tuple-element.12.refs_2_), channel_id=1, source_target_pairs={{0,4},{4,0},{8,12},{12,8},{1,5},{5,1},{9,13},{13,9},{2,6},{6,2},{1... | collective-permute-start | bytes 393224 | tf_op jit(solution)/shard_map/ppermute | solution.py:80
  5.5 2.6 %collective-permute-start.1 = (bf16[512,128]{1,0:T(8,128)(2,1)}, bf16[512,128]{1,0:T(8,128)(2,1)S(1)}, u32[]{:S(2)}, u32[]{:S(2)}) collective-permute-start(bf16[512,128]{1,0:T(8,128)(2,1)} %get-tuple-element.12.refs_2_), channel_id=1, source_target_pairs={{0,8},{4,12},{8,0},{12,4},{1,9},{5,13},{9,1},{13,5},{2,10},{6,14},... | collective-permute-start | bytes 393224 | tf_op jit(solution)/shard_map/ppermute | solution.py:80
  8.1 1.0 %slice.3 = bf16[1,256,640]{2,1,0:T(8,128)(2,1)S(1)} slice(bf16[1,256,1280]{2,1,0:T(8,128)(2,1)} %refs_1_.3), slice={[0:1], [0:256], [640:1280]} | slice | bytes 655360 | tf_op jit(solution)/shard_map/slice | solution.py:388
  9.1 1.8 %collective-permute-start.5 = (bf16[1,256,640]{2,1,0:T(8,128)(2,1)S(1)}, bf16[1,256,640]{2,1,0:T(8,128)(2,1)S(1)}, u32[]{:S(2)}, u32[]{:S(2)}) collective-permute-start(bf16[1,256,640]{2,1,0:T(8,128)(2,1)S(1)} %slice.3), channel_id=1, source_target_pairs={{0,2},{2,0},{1,3},{3,1},{4,6},{6,4},{5,7},{7,5},{8,10},{10,8},{9,1... | collective-permute-start | bytes 983048 | tf_op jit(solution)/shard_map/ppermute | solution.py:380
  10.9 0.1 pad_add_fusion.refs_0_
  10.9 0.5 stage.1.refs_6_
  11.5 7.1 %collective-permute-done.1.refs_4_ = bf16[512,128]{1,0:T(8,128)(2,1)S(1)} collective-permute-done((bf16[512,128]{1,0:T(8,128)(2,1)}, bf16[512,128]{1,0:T(8,128)(2,1)S(1)}, u32[]{:S(2)}, u32[]{:S(2)}) %collective-permute-start.1) | collective-permute-done | bytes 131104 | tf_op jit(solution)/shard_map/ppermute | solution.py:80
  18.6 0.0 collective-permute-done.2.refs_5_
  18.6 2.8 %attend.2 = bf16[1,256,640]{2,1,0:T(8,128)(2,1)S(1)} custom-call(s32[1,7]{1,0:T(1,128)S(1)} %pad_add_fusion.refs_0_, bf16[1,256,1280]{2,1,0:T(8,128)(2,1)S(1)} %copy-done, bf16[512,128]{1,0:T(8,128)(2,1)S(1)} %copy-done.1, bf16[512,128]{1,0:T(8,128)(2,1)S(1)} %collective-permute-done.refs_3_, bf16[512,128]{1,0:T(8,128)(2,1)S(1)} %collective-permute-done.1.refs_4_, ...), custom_call_target="tpu_custom_call" | custom-call | flops 419430400 | bytes 1179648 | tf_op jit(solution)/shard_map/attend/pallas_call | solution.py:212
  21.4 1.6 %collective-permute-start.3 = (bf16[1,256,640]{2,1,0:T(8,128)(2,1)S(1)}, bf16[1,256,640]{2,1,0:T(8,128)(2,1)S(1)}, u32[]{:S(2)}, u32[]{:S(2)}) collective-permute-start(bf16[1,256,640]{2,1,0:T(8,128)(2,1)S(1)} %attend.2), channel_id=1, source_target_pairs={{0,2},{2,0},{1,3},{3,1},{4,6},{6,4},{5,7},{7,5},{8,10},{10,8},{9,1... | collective-permute-start | bytes 983048 | tf_op jit(solution)/shard_map/ppermute | solution.py:380
  23.0 0.5 collective-permute-start.6
  23.5 2.4 %pack_pages.1 = (bf16[256,128]{1,0:T(8,128)(2,1)}, bf16[256,128]{1,0:T(8,128)(2,1)}, bf16[256,128]{1,0:T(8,128)(2,1)}) custom-call(s32[1,4]{1,0:T(1,128)} %refs_0_.3, s32[64]{0:T(128)} %bitcast.1, bf16[512,128]{1,0:T(8,128)(2,1)} %get-tuple-element.13.refs_6_.refs_2_), custom_call_target="tpu_custom_call" | custom-call | tf_op jit(solution)/shard_map/pack_pages/pallas_call | solution.py:278
  25.9 3.0 %collective-permute-start.10 = (bf16[256,128]{1,0:T(8,128)(2,1)}, bf16[256,128]{1,0:T(8,128)(2,1)S(1)}, u32[]{:S(2)}, u32[]{:S(2)}) collective-permute-start(bf16[256,128]{1,0:T(8,128)(2,1)} %get-tuple-element.16), channel_id=1, source_target_pairs={{0,4},{4,0},{8,12},{12,8},{1,5},{5,1},{9,13},{13,9},{2,6},{6,2},{1... | collective-permute-start | bytes 196616 | tf_op jit(solution)/shard_map/ppermute | solution.py:80
  28.9 0.5 collective-permute-start.4
  29.4 3.1 %collective-permute-done.4.refs_0_ = s32[1,7]{1,0:T(1,128)S(1)} collective-permute-done((s32[1,7]{1,0:T(1,128)S(1)}, s32[1,7]{1,0:T(1,128)S(1)}, u32[]{:S(2)}, u32[]{:S(2)}) %collective-permute-start.4) | collective-permute-done | bytes 60 | tf_op jit(solution)/shard_map/ppermute | solution.py:380
  32.5 3.5 %collective-permute-start.11 = (bf16[256,128]{1,0:T(8,128)(2,1)}, bf16[256,128]{1,0:T(8,128)(2,1)S(1)}, u32[]{:S(2)}, u32[]{:S(2)}) collective-permute-start(bf16[256,128]{1,0:T(8,128)(2,1)} %get-tuple-element.17), channel_id=1, source_target_pairs={{0,8},{4,12},{8,0},{12,4},{1,9},{5,13},{9,1},{13,5},{2,10},{6,14},... | collective-permute-start | bytes 196616 | tf_op jit(solution)/shard_map/ppermute | solution.py:80
  36.0 0.0 collective-permute-done.10.refs_2_
  36.0 2.2 %collective-permute-start.12 = (bf16[256,128]{1,0:T(8,128)(2,1)}, bf16[256,128]{1,0:T(8,128)(2,1)S(1)}, u32[]{:S(2)}, u32[]{:S(2)}) collective-permute-start(bf16[256,128]{1,0:T(8,128)(2,1)} %get-tuple-element.18), channel_id=1, source_target_pairs={{0,12},{4,8},{8,4},{12,0},{1,13},{5,9},{9,5},{13,1},{2,14},{6,10},... | collective-permute-start | bytes 196616 | tf_op jit(solution)/shard_map/ppermute | solution.py:80
  38.2 0.0 collective-permute-done.6.refs_2_
  38.2 0.0 collective-permute-start.7
  38.2 1.1 %collective-permute-done.11.refs_3_ = bf16[256,128]{1,0:T(8,128)(2,1)S(1)} collective-permute-done((bf16[256,128]{1,0:T(8,128)(2,1)}, bf16[256,128]{1,0:T(8,128)(2,1)S(1)}, u32[]{:S(2)}, u32[]{:S(2)}) %collective-permute-start.11) | collective-permute-done | bytes 65568 | tf_op jit(solution)/shard_map/ppermute | solution.py:80
  39.3 2.8 %collective-permute-start.8 = (bf16[512,128]{1,0:T(8,128)(2,1)S(1)}, bf16[512,128]{1,0:T(8,128)(2,1)S(1)}, u32[]{:S(2)}, u32[]{:S(2)}) collective-permute-start(bf16[512,128]{1,0:T(8,128)(2,1)S(1)} %collective-permute-done.6.refs_2_), channel_id=1, source_target_pairs={{0,8},{4,12},{8,0},{12,4},{1,9},{5,13},{9,1},{13,5},{2,10},{6,14},... | collective-permute-start | bytes 393224 | tf_op jit(solution)/shard_map/ppermute | solution.py:80
  42.1 1.0 %collective-permute-done.12.refs_4_ = bf16[256,128]{1,0:T(8,128)(2,1)S(1)} collective-permute-done((bf16[256,128]{1,0:T(8,128)(2,1)}, bf16[256,128]{1,0:T(8,128)(2,1)S(1)}, u32[]{:S(2)}, u32[]{:S(2)}) %collective-permute-start.12) | collective-permute-done | bytes 65568 | tf_op jit(solution)/shard_map/ppermute | solution.py:80
  43.1 2.1 %collective-permute-start.9 = (bf16[512,128]{1,0:T(8,128)(2,1)S(1)}, bf16[512,128]{1,0:T(8,128)(2,1)S(1)}, u32[]{:S(2)}, u32[]{:S(2)}) collective-permute-start(bf16[512,128]{1,0:T(8,128)(2,1)S(1)} %collective-permute-done.6.refs_2_), channel_id=1, source_target_pairs={{0,12},{4,8},{8,4},{12,0},{1,13},{5,9},{9,5},{13,1},{2,14},{6,10},... | collective-permute-start | bytes 393224 | tf_op jit(solution)/shard_map/ppermute | solution.py:80
  45.1 3.3 %scatter_pages.1 = (bf16[1,1,512,256]{3,2,1,0:T(8,128)(2,1)}, bf16[1,1,512,256]{3,2,1,0:T(8,128)(2,1)}) custom-call(s32[1,4]{1,0:T(1,128)} %refs_0_.3, s32[64]{0:T(128)} %bitcast.2, bf16[512,128]{1,0:T(8,128)(2,1)} %get-tuple-element.12.refs_2_, bf16[512,128]{1,0:T(8,128)(2,1)} %copy-done.2, bf16[512,128]{1,0:T(8,128)(2,1)} %copy-done.3, ...), custom_call_target="tpu_custom_call" | custom-call | tf_op jit(solution)/shard_map/scatter_pages/pallas_call | solution.py:313
  48.4 0.7 %land_pages.1 = (bf16[1,1,512,256]{3,2,1,0:T(8,128)(2,1)}, bf16[1,1,512,256]{3,2,1,0:T(8,128)(2,1)}) custom-call(bf16[1,1,512,256]{3,2,1,0:T(8,128)(2,1)} %get-tuple-element.14.refs_0_, bf16[1,1,512,256]{3,2,1,0:T(8,128)(2,1)} %get-tuple-element.15.refs_1_, ...), custom_call_target="tpu_custom_call", output_to_operand_aliasing={{0}: (0, {}), {1}: (1, {})} | custom-call | tf_op jit(solution)/shard_map/land_pages/pallas_call | solution.py:351
  49.2 1.6 %collective-permute-done.8.refs_4_ = bf16[512,128]{1,0:T(8,128)(2,1)S(1)} collective-permute-done((bf16[512,128]{1,0:T(8,128)(2,1)S(1)}, bf16[512,128]{1,0:T(8,128)(2,1)S(1)}, u32[]{:S(2)}, u32[]{:S(2)}) %collective-permute-start.8) | collective-permute-done | bytes 131104 | tf_op jit(solution)/shard_map/ppermute | solution.py:80
  50.7 2.9 %attend.3 = bf16[1,256,640]{2,1,0:T(8,128)(2,1)S(1)} custom-call(s32[1,7]{1,0:T(1,128)S(1)} %collective-permute-done.4.refs_0_, bf16[1,256,640]{2,1,0:T(8,128)(2,1)S(1)} %collective-permute-done.5.refs_1_, bf16[512,128]{1,0:T(8,128)(2,1)S(1)} %collective-permute-done.6.refs_2_, bf16[512,128]{1,0:T(8,128)(2,1)S(1)} %collective-permute-done.7.refs_3_, ...), custom_call_target="tpu_custom_call" | custom-call | flops 419430400 | bytes 1179648 | tf_op jit(solution)/shard_map/attend/pallas_call | solution.py:212
  53.6 0.9 %pad_maximum_fusion = bf16[1,256,1280]{2,1,0:T(8,128)(2,1)} fusion(bf16[1,256,640]{2,1,0:T(8,128)(2,1)S(1)} %attend.3, bf16[1,256,640]{2,1,0:T(8,128)(2,1)S(1)} %collective-permute-done.3), kind=kLoop, calls=%fused_computation | loop fusion | flops 1310720 | bytes 1310720 | tf_op jit(solution)/shard_map/concatenate | solution.py:411
  (20 shorter events, 0.0 us)
Async XLA Ops:
  0.6 10.3 %copy-start = (bf16[1,256,1280]{2,1,0:T(8,128)(2,1)S(1)}, bf16[1,256,1280]{2,1,0:T(8,128)(2,1)}, u32[]{:S(2)}) copy-start(bf16[1,256,1280]{2,1,0:T(8,128)(2,1)} %refs_1_.3) | copy-start | bytes 1966084
  0.6 10.2 %copy-start.6 = (s32[1,4]{1,0:T(1,128)S(1)}, s32[1,4]{1,0:T(1,128)}, u32[]{:S(2)}) copy-start(s32[1,4]{1,0:T(1,128)} %refs_0_.3) | copy-start | bytes 52
  0.7 10.2 %copy-start.7 = (s32[1,3]{1,0:T(1,128)S(1)}, s32[1,3]{1,0:T(1,128)}, u32[]{:S(2)}) copy-start(s32[1,3]{1,0:T(1,128)} %param.9) | copy-start | bytes 40
  2.4 8.5 %copy-start.1 = (bf16[512,128]{1,0:T(8,128)(2,1)S(1)}, bf16[512,128]{1,0:T(8,128)(2,1)}, u32[]{:S(2)}) copy-start(bf16[512,128]{1,0:T(8,128)(2,1)} %get-tuple-element.12.refs_2_) | copy-start | bytes 393220
  2.4 9.1 %collective-permute-start = (bf16[512,128]{1,0:T(8,128)(2,1)}, bf16[512,128]{1,0:T(8,128)(2,1)S(1)}, u32[]{:S(2)}, u32[]{:S(2)}) collective-permute-start(bf16[512,128]{1,0:T(8,128)(2,1)} %get-tuple-element.12.refs_2_), channel_id=1, source_target_pairs={{0,4},{4,0},{8,12},{12,8},{1,5},{5,1},{9,13},{13,9},{2,6},{6,2},{1... | collective-permute-start | bytes 393224 | tf_op jit(solution)/shard_map/ppermute | solution.py:80
  5.5 13.1 %collective-permute-start.1 = (bf16[512,128]{1,0:T(8,128)(2,1)}, bf16[512,128]{1,0:T(8,128)(2,1)S(1)}, u32[]{:S(2)}, u32[]{:S(2)}) collective-permute-start(bf16[512,128]{1,0:T(8,128)(2,1)} %get-tuple-element.12.refs_2_), channel_id=1, source_target_pairs={{0,8},{4,12},{8,0},{12,4},{1,9},{5,13},{9,1},{13,5},{2,10},{6,14},... | collective-permute-start | bytes 393224 | tf_op jit(solution)/shard_map/ppermute | solution.py:80
  8.1 10.5 %collective-permute-start.2 = (bf16[512,128]{1,0:T(8,128)(2,1)}, bf16[512,128]{1,0:T(8,128)(2,1)S(1)}, u32[]{:S(2)}, u32[]{:S(2)}) collective-permute-start(bf16[512,128]{1,0:T(8,128)(2,1)} %get-tuple-element.12.refs_2_), channel_id=1, source_target_pairs={{0,12},{4,8},{8,4},{12,0},{1,13},{5,9},{9,5},{13,1},{2,14},{6,10},... | collective-permute-start | bytes 393224 | tf_op jit(solution)/shard_map/ppermute | solution.py:80
  9.1 41.6 %collective-permute-start.5 = (bf16[1,256,640]{2,1,0:T(8,128)(2,1)S(1)}, bf16[1,256,640]{2,1,0:T(8,128)(2,1)S(1)}, u32[]{:S(2)}, u32[]{:S(2)}) collective-permute-start(bf16[1,256,640]{2,1,0:T(8,128)(2,1)S(1)} %slice.3), channel_id=1, source_target_pairs={{0,2},{2,0},{1,3},{3,1},{4,6},{6,4},{5,7},{7,5},{8,10},{10,8},{9,1... | collective-permute-start | bytes 983048 | tf_op jit(solution)/shard_map/ppermute | solution.py:380
  11.5 11.5 %copy-start.5 = (bf16[512,128]{1,0:T(8,128)(2,1)S(1)}, bf16[512,128]{1,0:T(8,128)(2,1)}, u32[]{:S(2)}) copy-start(bf16[512,128]{1,0:T(8,128)(2,1)} %get-tuple-element.13.refs_6_.refs_2_) | copy-start | bytes 393220
  11.5 9.9 %copy-start.2 = (bf16[512,128]{1,0:T(8,128)(2,1)}, bf16[512,128]{1,0:T(8,128)(2,1)S(1)}, u32[]{:S(2)}) copy-start(bf16[512,128]{1,0:T(8,128)(2,1)S(1)} %collective-permute-done.refs_3_) | copy-start | bytes 393220
  18.6 2.9 %copy-start.3 = (bf16[512,128]{1,0:T(8,128)(2,1)}, bf16[512,128]{1,0:T(8,128)(2,1)S(1)}, u32[]{:S(2)}) copy-start(bf16[512,128]{1,0:T(8,128)(2,1)S(1)} %collective-permute-done.1.refs_4_) | copy-start | bytes 393220
  18.6 2.9 %copy-start.4 = (bf16[512,128]{1,0:T(8,128)(2,1)}, bf16[512,128]{1,0:T(8,128)(2,1)S(1)}, u32[]{:S(2)}) copy-start(bf16[512,128]{1,0:T(8,128)(2,1)S(1)} %collective-permute-done.2.refs_5_) | copy-start | bytes 393220
  21.4 32.2 %collective-permute-start.3 = (bf16[1,256,640]{2,1,0:T(8,128)(2,1)S(1)}, bf16[1,256,640]{2,1,0:T(8,128)(2,1)S(1)}, u32[]{:S(2)}, u32[]{:S(2)}) collective-permute-start(bf16[1,256,640]{2,1,0:T(8,128)(2,1)S(1)} %attend.2), channel_id=1, source_target_pairs={{0,2},{2,0},{1,3},{3,1},{4,6},{6,4},{5,7},{7,5},{8,10},{10,8},{9,1... | collective-permute-start | bytes 983048 | tf_op jit(solution)/shard_map/ppermute | solution.py:380
  23.0 15.2 %collective-permute-start.6 = (bf16[512,128]{1,0:T(8,128)(2,1)S(1)}, bf16[512,128]{1,0:T(8,128)(2,1)S(1)}, u32[]{:S(2)}, u32[]{:S(2)}) collective-permute-start(bf16[512,128]{1,0:T(8,128)(2,1)S(1)} %copy-done.5), channel_id=1, source_target_pairs={{0,2},{2,0},{1,3},{3,1},{4,6},{6,4},{5,7},{7,5},{8,10},{10,8},{9,1... | collective-permute-start | bytes 393224 | tf_op jit(solution)/shard_map/ppermute | solution.py:380
  25.9 10.1 %collective-permute-start.10 = (bf16[256,128]{1,0:T(8,128)(2,1)}, bf16[256,128]{1,0:T(8,128)(2,1)S(1)}, u32[]{:S(2)}, u32[]{:S(2)}) collective-permute-start(bf16[256,128]{1,0:T(8,128)(2,1)} %get-tuple-element.16), channel_id=1, source_target_pairs={{0,4},{4,0},{8,12},{12,8},{1,5},{5,1},{9,13},{13,9},{2,6},{6,2},{1... | collective-permute-start | bytes 196616 | tf_op jit(solution)/shard_map/ppermute | solution.py:80
  28.9 3.6 %collective-permute-start.4 = (s32[1,7]{1,0:T(1,128)S(1)}, s32[1,7]{1,0:T(1,128)S(1)}, u32[]{:S(2)}, u32[]{:S(2)}) collective-permute-start(s32[1,7]{1,0:T(1,128)S(1)} %pad_add_fusion.refs_0_), channel_id=1, source_target_pairs={{0,2},{2,0},{1,3},{3,1},{4,6},{6,4},{5,7},{7,5},{8,10},{10,8},{9,1... | collective-permute-start | bytes 92 | tf_op jit(solution)/shard_map/ppermute | solution.py:380
  32.5 6.8 %collective-permute-start.11 = (bf16[256,128]{1,0:T(8,128)(2,1)}, bf16[256,128]{1,0:T(8,128)(2,1)S(1)}, u32[]{:S(2)}, u32[]{:S(2)}) collective-permute-start(bf16[256,128]{1,0:T(8,128)(2,1)} %get-tuple-element.17), channel_id=1, source_target_pairs={{0,8},{4,12},{8,0},{12,4},{1,9},{5,13},{9,1},{13,5},{2,10},{6,14},... | collective-permute-start | bytes 196616 | tf_op jit(solution)/shard_map/ppermute | solution.py:80
  36.0 7.1 %collective-permute-start.12 = (bf16[256,128]{1,0:T(8,128)(2,1)}, bf16[256,128]{1,0:T(8,128)(2,1)S(1)}, u32[]{:S(2)}, u32[]{:S(2)}) collective-permute-start(bf16[256,128]{1,0:T(8,128)(2,1)} %get-tuple-element.18), channel_id=1, source_target_pairs={{0,12},{4,8},{8,4},{12,0},{1,13},{5,9},{9,5},{13,1},{2,14},{6,10},... | collective-permute-start | bytes 196616 | tf_op jit(solution)/shard_map/ppermute | solution.py:80
  38.2 11.0 %collective-permute-start.7 = (bf16[512,128]{1,0:T(8,128)(2,1)S(1)}, bf16[512,128]{1,0:T(8,128)(2,1)S(1)}, u32[]{:S(2)}, u32[]{:S(2)}) collective-permute-start(bf16[512,128]{1,0:T(8,128)(2,1)S(1)} %collective-permute-done.6.refs_2_), channel_id=1, source_target_pairs={{0,4},{4,0},{8,12},{12,8},{1,5},{5,1},{9,13},{13,9},{2,6},{6,2},{1... | collective-permute-start | bytes 393224 | tf_op jit(solution)/shard_map/ppermute | solution.py:80
  39.3 11.4 %collective-permute-start.8 = (bf16[512,128]{1,0:T(8,128)(2,1)S(1)}, bf16[512,128]{1,0:T(8,128)(2,1)S(1)}, u32[]{:S(2)}, u32[]{:S(2)}) collective-permute-start(bf16[512,128]{1,0:T(8,128)(2,1)S(1)} %collective-permute-done.6.refs_2_), channel_id=1, source_target_pairs={{0,8},{4,12},{8,0},{12,4},{1,9},{5,13},{9,1},{13,5},{2,10},{6,14},... | collective-permute-start | bytes 393224 | tf_op jit(solution)/shard_map/ppermute | solution.py:80
  43.1 7.6 %collective-permute-start.9 = (bf16[512,128]{1,0:T(8,128)(2,1)S(1)}, bf16[512,128]{1,0:T(8,128)(2,1)S(1)}, u32[]{:S(2)}, u32[]{:S(2)}) collective-permute-start(bf16[512,128]{1,0:T(8,128)(2,1)S(1)} %collective-permute-done.6.refs_2_), channel_id=1, source_target_pairs={{0,12},{4,8},{8,4},{12,0},{1,13},{5,9},{9,5},{13,1},{2,14},{6,10},... | collective-permute-start | bytes 393224 | tf_op jit(solution)/shard_map/ppermute | solution.py:80
where the time goes:
time: 54.7 us; the launch traced here: 54.5 us
  starting transfers between devices  23.6 us (43%)
  Pallas kernels  14.4 us (26%)
  waiting for transfers between devices  13.8 us (25%)
  local copies, waits for them, and re-layouts  1.04 us (2%)
  other arithmetic  0.96 us (2%)
  between operations  0.77 us (1%)
    ppermute x9, starting transfers between devices, exchange(): received.append(lax.ppermute(parts[turn - 1], 'seq', route))  19.2 us
    ppermute x9, waiting for transfers between devices, exchange(): received.append(lax.ppermute(parts[turn - 1], 'seq', route))  10.7 us
    pallas_call x2, Pallas kernels, attend(): pl.pallas_call(kernel, out_shape=jax.ShapeDtypeStruct((1, rows, width), q...  5.72 us
    ppermute x4, starting transfers between devices, hand_on(): return lax.ppermute(array, 'section', onward)  4.36 us
    pallas_call x1, Pallas kernels, scatter_pages(): pl.pallas_call(kernel, out_shape=[cache, cache], in_specs=[SMEM, SMEM] +...  3.27 us
    ppermute x4, waiting for transfers between devices, hand_on(): return lax.ppermute(array, 'section', onward)  3.08 us
    pallas_call x1, Pallas kernels, pack_pages(): pl.pallas_call(kernel, out_shape=[part] * (count - 1), in_specs=[SMEM, SM...  2.39 us
    pallas_call x1, Pallas kernels, split_heads(): pl.pallas_call(split_heads_kernel, out_shape=[message] * (width // HEAD_S...  1.76 us
  transfers between devices with their start and end apart: 13, of which 5 were waited for; matrix products, arithmetic and copies ran while one was open for 2% of the time, Pallas kernels for 23%

commit v1 on v0

--- a/solution.py
+++ b/solution.py
@@ -234,43 +234,40 @@
     )(plan, queries, *blocks, staged)
 
 
-def for_owner(order_ref, owner_ref, source, owner, pages, act):
-    block = order_ref[0, source]
-
-    def page_step(page, rank):
-        wanted = owner_ref[block * pages + page] == owner
-        pl.when(wanted)(lambda: act(page, rank))
-        return rank + wanted.astype(jnp.int32)
-
-    lax.fori_loop(0, pages, page_step, jnp.int32(0))
-
-
 def page_rows(page, page_tokens, base=0):
-    return pl.ds(pl.multiple_of(base + page * page_tokens, page_tokens), page_tokens)
-
-
-def pack_kernel(order_ref, owner_ref, message_ref, *part_refs, page_tokens):
+    start = base + page * page_tokens
+    return pl.ds(start if isinstance(start, int) else pl.multiple_of(start, page_tokens), page_tokens)
+
+
+def pack_kernel(order_ref, owner_ref, message_ref, *refs, page_tokens):
+    part_refs, buffer_ref = refs[:-1], refs[-1]
     count = len(part_refs) + 1
     rows = message_ref.shape[0] // 2
     half = part_refs[0].shape[0] // 2
+    pages = rows // page_tokens
     own = lax.axis_index("seq")
+    block = order_ref[0, own]
+    buffer_ref[...] = jnp.zeros_like(buffer_ref)
+    taken = [jnp.int32(0)] * count
+    for page in range(pages):
+        owner = owner_ref[block * pages + page]
+        rank = jnp.int32(0)
+        for index in range(count):
+            same = owner == index
+            rank = jnp.where(same, taken[index], rank)
+            taken[index] = taken[index] + same.astype(jnp.int32)
+        for base, part_base in ((0, 0), (rows, half)):
+            buffer_ref[owner, page_rows(rank, page_tokens, part_base), :] = message_ref[
+                page_rows(page, page_tokens, base), :
+            ]
     for turn in range(1, count):
-        part_ref = part_refs[turn - 1]
-        part_ref[...] = jnp.zeros_like(part_ref)
-
-        def act(page, rank):
-            for base, part_base in ((0, 0), (rows, half)):
-                part_ref[page_rows(rank, page_tokens, part_base), :] = message_ref[
-                    page_rows(page, page_tokens, base), :
-                ]
-
-        owner = partner_of(own, turn, count)
-        for_owner(order_ref, owner_ref, own, owner, rows // page_tokens, act)
+        part_refs[turn - 1][...] = buffer_ref[partner_of(own, turn, count)]
 
 
 def pack_pages(block_order, owners, message, slots, page_tokens):
     count = block_order.shape[1]
-    part = jax.ShapeDtypeStruct((2 * slots * page_tokens, HEAD_SIZE), message.dtype)
+    shape = (2 * slots * page_tokens, HEAD_SIZE)
+    part = jax.ShapeDtypeStruct(shape, message.dtype)
 
     def kernel(*refs):
         pack_kernel(*refs, page_tokens=page_tokens)
@@ -280,32 +277,41 @@
         out_shape=[part] * (count - 1),
         in_specs=[SMEM, SMEM, VMEM],
         out_specs=[VMEM] * (count - 1),
+        scratch_shapes=[pltpu.VMEM((count, *shape), message.dtype)],
         name="pack_pages",
     )(block_order, owners, message)
 
 
 def scatter_kernel(order_ref, owner_ref, *refs, columns, page_tokens, slots):
-    keys_ref, values_ref = refs[-2:]
-    keys_ref[...] = jnp.zeros_like(keys_ref)
-    values_ref[...] = jnp.zeros_like(values_ref)
+    keys_ref, values_ref, held_keys_ref, held_values_ref = refs[-4:]
+    total = keys_ref.shape[2]
+    held_keys_ref[...] = jnp.zeros_like(held_keys_ref)
+    held_values_ref[...] = jnp.zeros_like(held_values_ref)
     own = lax.axis_index("seq")
     count = order_ref.shape[1]
-    for block_ref, (head, turn) in zip(refs[:-2], columns):
-        rows = block_ref.shape[0] // 2
+    for turn in range(count):
         source = source_of(own, turn, count)
-        lanes = pl.ds(head * HEAD_SIZE, HEAD_SIZE)
-
-        def act(page, rank):
-            put = page_rows(source * slots + rank, page_tokens)
-            keys_ref[0, 0, put, lanes] = block_ref[page_rows(page, page_tokens), :]
-            values_ref[0, 0, put, lanes] = block_ref[page_rows(page, page_tokens, rows), :]
-
-        for_owner(order_ref, owner_ref, source, own, rows // page_tokens, act)
+        block = order_ref[0, source]
+        heads = [(ref, head) for ref, (head, at) in zip(refs[:-4], columns) if at == turn]
+        rows = heads[0][0].shape[0] // 2
+        pages = rows // page_tokens
+        rank = source * slots
+        for page in range(pages):
+            mine = owner_ref[block * pages + page] == own
+            put = page_rows(jnp.where(mine, rank, total // page_tokens), page_tokens)
+            rank = rank + mine.astype(jnp.int32)
+            for block_ref, head in heads:
+                lanes = pl.ds(head * HEAD_SIZE, HEAD_SIZE)
+                held_keys_ref[put, lanes] = block_ref[page_rows(page, page_tokens), :]
+                held_values_ref[put, lanes] = block_ref[page_rows(page, page_tokens, rows), :]
+    keys_ref[0, 0] = held_keys_ref[:total, :]
+    values_ref[0, 0] = held_values_ref[:total, :]
 
 
 def scatter_pages(block_order, owners, blocks, columns, width, page_tokens, slots):
     count = block_order.shape[1]
-    cache = jax.ShapeDtypeStruct((1, 1, count * slots * page_tokens, width), blocks[0].dtype)
+    total = count * slots * page_tokens
+    cache = jax.ShapeDtypeStruct((1, 1, total, width), blocks[0].dtype)
 
     def kernel(*refs):
         scatter_kernel(*refs, columns=columns, page_tokens=page_tokens, slots=slots)
@@ -315,51 +321,63 @@
         out_shape=[cache, cache],
         in_specs=[SMEM, SMEM] + [VMEM] * len(blocks),
         out_specs=[VMEM, VMEM],
+        scratch_shapes=[pltpu.VMEM((total + page_tokens, width), blocks[0].dtype)] * 2,
         name="scatter_pages",
     )(block_order, owners, *blocks)
 
 
-def land_kernel(keys_in_ref, values_in_ref, *refs, head):
-    keys_ref, values_ref, sems = refs[-3:]
-    part_refs = refs[:-3]
-    count = len(part_refs) + 1
+def finish_kernel(*refs, contexts, heads):
+    count = lax.axis_size("seq")
+    context_refs = refs[2 : 2 + contexts]
+    part_refs = refs[2 + contexts : -4]
+    keys_ref, values_ref, handed_ref, sems = refs[-4:]
     half = part_refs[0].shape[0] // 2
     own = lax.axis_index("seq")
-    lanes = pl.ds(head * HEAD_SIZE, HEAD_SIZE)
     copies = []
-    for turn in range(1, count):
-        source = source_of(own, turn, count)
+    start = 0
+    for context_ref in context_refs:
+        width = context_ref.shape[2]
+        copies.append((context_ref, handed_ref.at[:, :, pl.ds(start, width)]))
+        start += width
+    for index, part_ref in enumerate(part_refs):
+        lanes = pl.ds(heads[index // (count - 1)] * HEAD_SIZE, HEAD_SIZE)
+        source = source_of(own, index % (count - 1) + 1, count)
         put = pl.ds(pl.multiple_of(source * half, half), half)
         for side, cache_ref in enumerate((keys_ref, values_ref)):
             copies.append(
-                pltpu.make_async_copy(
-                    part_refs[turn - 1].at[pl.ds(side * half, half), :],
-                    cache_ref.at[0, 0, put, lanes],
-                    sems.at[2 * (turn - 1) + side],
-                )
+                (part_ref.at[pl.ds(side * half, half), :], cache_ref.at[0, 0, put, lanes])
             )
+    copies = [
+        pltpu.make_async_copy(source, target, sems.at[index])
+        for index, (source, target) in enumerate(copies)
+    ]
     for copy in copies:
         copy.start()
     for copy in copies:
         copy.wait()
 
 
-def land_pages(cache_keys, cache_values, parts, head):
+def finish(cache_keys, cache_values, contexts, parts, heads):
+    rows = contexts[0].shape[1]
+    width = sum(context.shape[2] for context in contexts)
+
     def kernel(*refs):
-        land_kernel(*refs, head=head)
-
+        finish_kernel(*refs, contexts=len(contexts), heads=heads)
+
+    outputs = [
+        jax.ShapeDtypeStruct(cache.shape, cache.dtype) for cache in (cache_keys, cache_values)
+    ]
+    outputs.append(jax.ShapeDtypeStruct((1, rows, width), contexts[0].dtype))
     return pl.pallas_call(
         kernel,
-        out_shape=[
-            jax.ShapeDtypeStruct(cache.shape, cache.dtype) for cache in (cache_keys, cache_values)
-        ],
-        in_specs=[ANY] * (2 + len(parts)),
-        out_specs=[ANY, ANY],
-        scratch_shapes=[pltpu.SemaphoreType.DMA((2 * len(parts),))],
+        out_shape=outputs,
+        in_specs=[ANY] * (2 + len(contexts) + len(parts)),
+        out_specs=[ANY] * 3,
+        scratch_shapes=[pltpu.SemaphoreType.DMA((len(contexts) + 2 * len(parts),))],
         input_output_aliases={0: 0, 1: 1},
         compiler_params=pltpu.CompilerParams(vmem_limit_bytes=48 * 2**20),
-        name="land_pages",
-    )(cache_keys, cache_values, *parts)
+        name="finish",
+    )(cache_keys, cache_values, *contexts, *parts)
 
 
 def body(queries, key_rows, values, lengths, block_order, page_owner):
@@ -392,7 +410,7 @@
     parts = []
     for head in range(kept, kv_heads):
         packed = pack_pages(block_order, owners, messages[head], slots, page_tokens)
-        parts.append(exchange(packed))
+        parts += exchange(packed)
     staged = stage(plan, queries, *messages[:kept])
     handed = []
     for head in range(kept):
@@ -406,9 +424,8 @@
     columns += [(head, 0) for head in range(kept, kv_heads)]
     blocks = [gathered[head][turn] if head < kept else messages[head] for head, turn in columns]
     cache = scatter_pages(block_order, owners, blocks, columns, width, page_tokens, slots)
-    for index, head in enumerate(range(kept, kv_heads)):
-        cache = land_pages(*cache, parts[index], head)
-    return (jnp.concatenate(handed, axis=2), *cache)
+    cache_keys, cache_values, context = finish(*cache, handed, parts, list(range(kept, kv_heads)))
+    return (context, cache_keys, cache_values)
 
 
 def solution(mesh):

time: 54.7 us -> 45.3 us (0.83)
  starting transfers between devices: 23.6 us -> 15.3 us
  Pallas kernels: 14.4 us -> 12.9 us
  waiting for transfers between devices: 13.8 us -> 15 us
  other arithmetic: 0.96 us -> 0.07 us
    ppermute x9, starting transfers between devices: 19.2 us -> 10.3 us  [exchange(): received.append(lax.ppermute(parts[turn - 1], 'seq', route))]
    ppermute x4, waiting for transfers between devices: 3.08 us -> 4.58 us  [hand_on(): return lax.ppermute(array, 'section', onward)]
    pallas_call x1, Pallas kernels: 3.27 us -> 2.19 us  [scatter_pages(): pl.pallas_call(kernel, out_shape=[cache, cache], in_specs=[SMEM, SMEM] +...]
    concatenate x1 -> x0, other arithmetic: 0.89 us -> none  [body(): return (jnp.concatenate(handed, axis=2), *cache)]
    pallas_call x1, Pallas kernels: 2.39 us -> 1.76 us  [pack_pages(): pl.pallas_call(kernel, out_shape=[part] * (count - 1), in_specs=[SMEM, SM...]
    ppermute x4, starting transfers between devices: 4.36 us -> 4.99 us  [hand_on(): return lax.ppermute(array, 'section', onward)]
  transfers between devices with their start and end apart: 13 -> 13, of which waited for: 5 -> 6; matrix products, arithmetic and copies ran while one was open for 2% -> 2% of each run, Pallas kernels for 23% -> 23%
where the time goes in v1:
time: 45.3 us; the launch traced here: 45.1 us
  starting transfers between devices  15.3 us (34%)
  waiting for transfers between devices  15 us (33%)
  Pallas kernels  12.9 us (28%)
  local copies, waits for them, and re-layouts  1.03 us (2%)
  between operations  0.72 us (2%)
    ppermute x9, waiting for transfers between devices, exchange(): received.append(lax.ppermute(parts[turn - 1], 'seq', route))  10.5 us
    ppermute x9, starting transfers between devices, exchange(): received.append(lax.ppermute(parts[turn - 1], 'seq', route))  10.3 us
    pallas_call x2, Pallas kernels, attend(): pl.pallas_call(kernel, out_shape=jax.ShapeDtypeStruct((1, rows, width), q...  5.73 us
    ppermute x4, starting transfers between devices, hand_on(): return lax.ppermute(array, 'section', onward)  4.99 us
    ppermute x4, waiting for transfers between devices, hand_on(): return lax.ppermute(array, 'section', onward)  4.58 us
    pallas_call x1, Pallas kernels, scatter_pages(): pl.pallas_call(kernel, out_shape=[cache, cache], in_specs=[SMEM, SMEM] +...  2.19 us
    pallas_call x1, Pallas kernels, split_heads(): pl.pallas_call(split_heads_kernel, out_shape=[message] * (width // HEAD_S...  1.77 us
    pallas_call x1, Pallas kernels, pack_pages(): pl.pallas_call(kernel, out_shape=[part] * (count - 1), in_specs=[SMEM, SM...  1.76 us
  transfers between devices with their start and end apart: 13, of which 6 were waited for; matrix products, arithmetic and copies ran while one was open for 2% of the time, Pallas kernels for 23%

profile of v1, /device:TPU:0, one launch (start us, length us, event | category | flops | bytes accessed | tf_op | source)
XLA Modules:
  0.0 45.1 jit_solution(1999445312921522600)
XLA Ops:
  0.6 0.0 copy-start
  0.6 1.8 %split_heads.1 = (bf16[512,128]{1,0:T(8,128)(2,1)}, bf16[512,128]{1,0:T(8,128)(2,1)}) custom-call(bf16[1,256,256]{2,1,0:T(8,128)(2,1)} %keys_ref.1, bf16[1,256,256]{2,1,0:T(8,128)(2,1)} %values_ref.1), custom_call_target="tpu_custom_call" | custom-call | tf_op jit(solution)/shard_map/split_heads/pallas_call | solution.py:51
  2.4 5.1 %collective-permute-start.2 = (bf16[512,128]{1,0:T(8,128)(2,1)}, bf16[512,128]{1,0:T(8,128)(2,1)S(1)}, u32[]{:S(2)}, u32[]{:S(2)}) collective-permute-start(bf16[512,128]{1,0:T(8,128)(2,1)} %get-tuple-element.13.refs_2_), channel_id=1, source_target_pairs={{0,12},{4,8},{8,4},{12,0},{1,13},{5,9},{9,5},{13,1},{2,14},{6,10},... | collective-permute-start | bytes 393224 | tf_op jit(solution)/shard_map/ppermute | solution.py:80
  7.5 0.6 %collective-permute-start = (bf16[512,128]{1,0:T(8,128)(2,1)}, bf16[512,128]{1,0:T(8,128)(2,1)S(1)}, u32[]{:S(2)}, u32[]{:S(2)}) collective-permute-start(bf16[512,128]{1,0:T(8,128)(2,1)} %get-tuple-element.13.refs_2_), channel_id=1, source_target_pairs={{0,4},{4,0},{8,12},{12,8},{1,5},{5,1},{9,13},{13,9},{2,6},{6,2},{1... | collective-permute-start | bytes 393224 | tf_op jit(solution)/shard_map/ppermute | solution.py:80
  8.1 1.7 %collective-permute-start.6 = (bf16[512,128]{1,0:T(8,128)(2,1)}, bf16[512,128]{1,0:T(8,128)(2,1)S(1)}, u32[]{:S(2)}, u32[]{:S(2)}) collective-permute-start(bf16[512,128]{1,0:T(8,128)(2,1)} %get-tuple-element.14.refs_6_.refs_2_), channel_id=1, source_target_pairs={{0,2},{2,0},{1,3},{3,1},{4,6},{6,4},{5,7},{7,5},{8,10},{10,8},{9,1... | collective-permute-start | bytes 393224 | tf_op jit(solution)/shard_map/ppermute | solution.py:398
  9.8 1.0 %slice.3 = bf16[1,256,640]{2,1,0:T(8,128)(2,1)S(1)} slice(bf16[1,256,1280]{2,1,0:T(8,128)(2,1)} %refs_1_.3), slice={[0:1], [0:256], [640:1280]} | slice | bytes 655360 | tf_op jit(solution)/shard_map/slice | solution.py:406
  10.8 0.4 collective-permute-start.5
  11.2 0.1 pad_add_fusion.refs_0_
  11.2 0.5 %stage.1.refs_6_ = f32[8,128]{1,0:T(8,128)S(1)} custom-call(s32[1,7]{1,0:T(1,128)S(1)} %pad_add_fusion.refs_0_, bf16[1,256,1280]{2,1,0:T(8,128)(2,1)S(1)} %copy-done, bf16[512,128]{1,0:T(8,128)(2,1)S(1)} %copy-done.1), custom_call_target="tpu_custom_call" | custom-call | tf_op jit(solution)/shard_map/stage/pallas_call | solution.py:65
  11.8 0.4 collective-permute-done.2.refs_5_
  12.2 6.6 %collective-permute-done.1.refs_4_ = bf16[512,128]{1,0:T(8,128)(2,1)S(1)} collective-permute-done((bf16[512,128]{1,0:T(8,128)(2,1)}, bf16[512,128]{1,0:T(8,128)(2,1)S(1)}, u32[]{:S(2)}, u32[]{:S(2)}) %collective-permute-start.1) | collective-permute-done | bytes 131104 | tf_op jit(solution)/shard_map/ppermute | solution.py:80
  18.8 0.0 collective-permute-done.refs_3_
  18.8 2.8 %attend.2 = bf16[1,256,640]{2,1,0:T(8,128)(2,1)S(1)} custom-call(s32[1,7]{1,0:T(1,128)S(1)} %pad_add_fusion.refs_0_, bf16[1,256,1280]{2,1,0:T(8,128)(2,1)S(1)} %copy-done, bf16[512,128]{1,0:T(8,128)(2,1)S(1)} %copy-done.1, bf16[512,128]{1,0:T(8,128)(2,1)S(1)} %collective-permute-done.refs_3_, bf16[512,128]{1,0:T(8,128)(2,1)S(1)} %collective-permute-done.1.refs_4_, ...), custom_call_target="tpu_custom_call" | custom-call | flops 419430400 | bytes 1179648 | tf_op jit(solution)/shard_map/attend/pallas_call | solution.py:212
  21.7 1.6 %collective-permute-start.3 = (bf16[1,256,640]{2,1,0:T(8,128)(2,1)S(1)}, bf16[1,256,640]{2,1,0:T(8,128)(2,1)S(1)}, u32[]{:S(2)}, u32[]{:S(2)}) collective-permute-start(bf16[1,256,640]{2,1,0:T(8,128)(2,1)S(1)} %attend.2), channel_id=1, source_target_pairs={{0,2},{2,0},{1,3},{3,1},{4,6},{6,4},{5,7},{7,5},{8,10},{10,8},{9,1... | collective-permute-start | bytes 983048 | tf_op jit(solution)/shard_map/ppermute | solution.py:398
  23.2 0.0 collective-permute-done.6.refs_2_
  23.2 1.5 %collective-permute-start.9 = (bf16[512,128]{1,0:T(8,128)(2,1)S(1)}, bf16[512,128]{1,0:T(8,128)(2,1)S(1)}, u32[]{:S(2)}, u32[]{:S(2)}) collective-permute-start(bf16[512,128]{1,0:T(8,128)(2,1)S(1)} %collective-permute-done.6.refs_2_), channel_id=1, source_target_pairs={{0,12},{4,8},{8,4},{12,0},{1,13},{5,9},{9,5},{13,1},{2,14},{6,10},... | collective-permute-start | bytes 393224 | tf_op jit(solution)/shard_map/ppermute | solution.py:80
  24.7 0.0 collective-permute-start.8
  24.7 1.3 %collective-permute-start.4 = (s32[1,7]{1,0:T(1,128)S(1)}, s32[1,7]{1,0:T(1,128)S(1)}, u32[]{:S(2)}, u32[]{:S(2)}) collective-permute-start(s32[1,7]{1,0:T(1,128)S(1)} %pad_add_fusion.refs_0_), channel_id=1, source_target_pairs={{0,2},{2,0},{1,3},{3,1},{4,6},{6,4},{5,7},{7,5},{8,10},{10,8},{9,1... | collective-permute-start | bytes 92 | tf_op jit(solution)/shard_map/ppermute | solution.py:398
  26.0 4.6 %collective-permute-done.4.refs_0_ = s32[1,7]{1,0:T(1,128)S(1)} collective-permute-done((s32[1,7]{1,0:T(1,128)S(1)}, s32[1,7]{1,0:T(1,128)S(1)}, u32[]{:S(2)}, u32[]{:S(2)}) %collective-permute-start.4) | collective-permute-done | bytes 60 | tf_op jit(solution)/shard_map/ppermute | solution.py:398
  30.6 0.7 %collective-permute-start.7 = (bf16[512,128]{1,0:T(8,128)(2,1)S(1)}, bf16[512,128]{1,0:T(8,128)(2,1)S(1)}, u32[]{:S(2)}, u32[]{:S(2)}) collective-permute-start(bf16[512,128]{1,0:T(8,128)(2,1)S(1)} %collective-permute-done.6.refs_2_), channel_id=1, source_target_pairs={{0,4},{4,0},{8,12},{12,8},{1,5},{5,1},{9,13},{13,9},{2,6},{6,2},{1... | collective-permute-start | bytes 393224 | tf_op jit(solution)/shard_map/ppermute | solution.py:80
  31.3 1.8 %pack_pages.1 = (bf16[256,128]{1,0:T(8,128)(2,1)}, bf16[256,128]{1,0:T(8,128)(2,1)}, bf16[256,128]{1,0:T(8,128)(2,1)}) custom-call(s32[1,4]{1,0:T(1,128)} %refs_0_.3, s32[64]{0:T(128)} %bitcast.1, bf16[512,128]{1,0:T(8,128)(2,1)} %get-tuple-element.14.refs_6_.refs_2_), custom_call_target="tpu_custom_call" | custom-call | tf_op jit(solution)/shard_map/pack_pages/pallas_call | solution.py:275
  33.0 0.0 collective-permute-done.9.refs_5_
  33.0 1.4 %collective-permute-start.10 = (bf16[256,128]{1,0:T(8,128)(2,1)}, bf16[256,128]{1,0:T(8,128)(2,1)S(1)}, u32[]{:S(2)}, u32[]{:S(2)}) collective-permute-start(bf16[256,128]{1,0:T(8,128)(2,1)} %get-tuple-element.17), channel_id=1, source_target_pairs={{0,4},{4,0},{8,12},{12,8},{1,5},{5,1},{9,13},{13,9},{2,6},{6,2},{1... | collective-permute-start | bytes 196616 | tf_op jit(solution)/shard_map/ppermute | solution.py:80
  34.5 1.5 %collective-permute-done.8.refs_4_ = bf16[512,128]{1,0:T(8,128)(2,1)S(1)} collective-permute-done((bf16[512,128]{1,0:T(8,128)(2,1)S(1)}, bf16[512,128]{1,0:T(8,128)(2,1)S(1)}, u32[]{:S(2)}, u32[]{:S(2)}) %collective-permute-start.8) | collective-permute-done | bytes 131104 | tf_op jit(solution)/shard_map/ppermute | solution.py:80
  36.0 1.9 %collective-permute-done.7.refs_3_ = bf16[512,128]{1,0:T(8,128)(2,1)S(1)} collective-permute-done((bf16[512,128]{1,0:T(8,128)(2,1)S(1)}, bf16[512,128]{1,0:T(8,128)(2,1)S(1)}, u32[]{:S(2)}, u32[]{:S(2)}) %collective-permute-start.7) | collective-permute-done | bytes 131104 | tf_op jit(solution)/shard_map/ppermute | solution.py:80
  37.8 1.0 %collective-permute-start.12 = (bf16[256,128]{1,0:T(8,128)(2,1)}, bf16[256,128]{1,0:T(8,128)(2,1)S(1)}, u32[]{:S(2)}, u32[]{:S(2)}) collective-permute-start(bf16[256,128]{1,0:T(8,128)(2,1)} %get-tuple-element.19), channel_id=1, source_target_pairs={{0,12},{4,8},{8,4},{12,0},{1,13},{5,9},{9,5},{13,1},{2,14},{6,10},... | collective-permute-start | bytes 196616 | tf_op jit(solution)/shard_map/ppermute | solution.py:80
  38.9 2.2 %scatter_pages.1 = (bf16[1,1,512,256]{3,2,1,0:T(8,128)(2,1)}, bf16[1,1,512,256]{3,2,1,0:T(8,128)(2,1)}) custom-call(s32[1,4]{1,0:T(1,128)} %refs_0_.3, s32[64]{0:T(128)} %bitcast.2, bf16[512,128]{1,0:T(8,128)(2,1)} %get-tuple-element.13.refs_2_, bf16[512,128]{1,0:T(8,128)(2,1)} %copy-done.4, bf16[512,128]{1,0:T(8,128)(2,1)} %copy-done.3, ...), custom_call_target="tpu_custom_call" | custom-call | tf_op jit(solution)/shard_map/scatter_pages/pallas_call | solution.py:319
  41.1 0.0 collective-permute-done.5.refs_1_
  41.1 2.9 %attend.3.refs_3_ = bf16[1,256,640]{2,1,0:T(8,128)(2,1)S(1)} custom-call(s32[1,7]{1,0:T(1,128)S(1)} %collective-permute-done.4.refs_0_, bf16[1,256,640]{2,1,0:T(8,128)(2,1)S(1)} %collective-permute-done.5.refs_1_, bf16[512,128]{1,0:T(8,128)(2,1)S(1)} %collective-permute-done.6.refs_2_, bf16[512,128]{1,0:T(8,128)(2,1)S(1)} %collective-permute-done.7.refs_3_, ...), custom_call_target="tpu_custom_call" | custom-call | flops 419430400 | bytes 1179648 | tf_op jit(solution)/shard_map/attend/pallas_call | solution.py:212
  44.0 0.0 collective-permute-done.11.refs_5_
  44.0 0.1 collective-permute-done.12.refs_6_
  44.1 1.0 %finish.1 = (bf16[1,1,512,256]{3,2,1,0:T(8,128)(2,1)}, bf16[1,1,512,256]{3,2,1,0:T(8,128)(2,1)}, bf16[1,256,1280]{2,1,0:T(8,128)(2,1)}) custom-call(bf16[1,1,512,256]{3,2,1,0:T(8,128)(2,1)} %get-tuple-element.15.refs_0_, bf16[1,1,512,256]{3,2,1,0:T(8,128)(2,1)} %get-tuple-element.16.refs_1_, ...), custom_call_target="tpu_custom_call", output_to_operand_aliasing={{0}: (0, {}), {1}: (1, {})} | custom-call | tf_op jit(solution)/shard_map/finish/pallas_call | solution.py:371
  (17 shorter events, 0.0 us)
Async XLA Ops:
  0.6 10.6 %copy-start = (bf16[1,256,1280]{2,1,0:T(8,128)(2,1)S(1)}, bf16[1,256,1280]{2,1,0:T(8,128)(2,1)}, u32[]{:S(2)}) copy-start(bf16[1,256,1280]{2,1,0:T(8,128)(2,1)} %refs_1_.3) | copy-start | bytes 1966084
  2.4 9.7 %collective-permute-start.2 = (bf16[512,128]{1,0:T(8,128)(2,1)}, bf16[512,128]{1,0:T(8,128)(2,1)S(1)}, u32[]{:S(2)}, u32[]{:S(2)}) collective-permute-start(bf16[512,128]{1,0:T(8,128)(2,1)} %get-tuple-element.13.refs_2_), channel_id=1, source_target_pairs={{0,12},{4,8},{8,4},{12,0},{1,13},{5,9},{9,5},{13,1},{2,14},{6,10},... | collective-permute-start | bytes 393224 | tf_op jit(solution)/shard_map/ppermute | solution.py:80
  7.5 11.3 %collective-permute-start.1 = (bf16[512,128]{1,0:T(8,128)(2,1)}, bf16[512,128]{1,0:T(8,128)(2,1)S(1)}, u32[]{:S(2)}, u32[]{:S(2)}) collective-permute-start(bf16[512,128]{1,0:T(8,128)(2,1)} %get-tuple-element.13.refs_2_), channel_id=1, source_target_pairs={{0,8},{4,12},{8,0},{12,4},{1,9},{5,13},{9,1},{13,5},{2,10},{6,14},... | collective-permute-start | bytes 393224 | tf_op jit(solution)/shard_map/ppermute | solution.py:80
  7.5 11.3 %collective-permute-start = (bf16[512,128]{1,0:T(8,128)(2,1)}, bf16[512,128]{1,0:T(8,128)(2,1)S(1)}, u32[]{:S(2)}, u32[]{:S(2)}) collective-permute-start(bf16[512,128]{1,0:T(8,128)(2,1)} %get-tuple-element.13.refs_2_), channel_id=1, source_target_pairs={{0,4},{4,0},{8,12},{12,8},{1,5},{5,1},{9,13},{13,9},{2,6},{6,2},{1... | collective-permute-start | bytes 393224 | tf_op jit(solution)/shard_map/ppermute | solution.py:80
  8.1 3.1 %copy-start.5 = (s32[1,4]{1,0:T(1,128)S(1)}, s32[1,4]{1,0:T(1,128)}, u32[]{:S(2)}) copy-start(s32[1,4]{1,0:T(1,128)} %refs_0_.3) | copy-start | bytes 52
  8.1 3.1 %copy-start.6 = (s32[1,3]{1,0:T(1,128)S(1)}, s32[1,3]{1,0:T(1,128)}, u32[]{:S(2)}) copy-start(s32[1,3]{1,0:T(1,128)} %param.9) | copy-start | bytes 40
  8.1 3.2 %copy-start.1 = (bf16[512,128]{1,0:T(8,128)(2,1)S(1)}, bf16[512,128]{1,0:T(8,128)(2,1)}, u32[]{:S(2)}) copy-start(bf16[512,128]{1,0:T(8,128)(2,1)} %get-tuple-element.13.refs_2_) | copy-start | bytes 393220
  8.1 15.1 %collective-permute-start.6 = (bf16[512,128]{1,0:T(8,128)(2,1)}, bf16[512,128]{1,0:T(8,128)(2,1)S(1)}, u32[]{:S(2)}, u32[]{:S(2)}) collective-permute-start(bf16[512,128]{1,0:T(8,128)(2,1)} %get-tuple-element.14.refs_6_.refs_2_), channel_id=1, source_target_pairs={{0,2},{2,0},{1,3},{3,1},{4,6},{6,4},{5,7},{7,5},{8,10},{10,8},{9,1... | collective-permute-start | bytes 393224 | tf_op jit(solution)/shard_map/ppermute | solution.py:398
  10.8 30.3 %collective-permute-start.5 = (bf16[1,256,640]{2,1,0:T(8,128)(2,1)S(1)}, bf16[1,256,640]{2,1,0:T(8,128)(2,1)S(1)}, u32[]{:S(2)}, u32[]{:S(2)}) collective-permute-start(bf16[1,256,640]{2,1,0:T(8,128)(2,1)S(1)} %slice.3), channel_id=1, source_target_pairs={{0,2},{2,0},{1,3},{3,1},{4,6},{6,4},{5,7},{7,5},{8,10},{10,8},{9,1... | collective-permute-start | bytes 983048 | tf_op jit(solution)/shard_map/ppermute | solution.py:398
  12.2 9.5 %copy-start.2 = (bf16[512,128]{1,0:T(8,128)(2,1)}, bf16[512,128]{1,0:T(8,128)(2,1)S(1)}, u32[]{:S(2)}) copy-start(bf16[512,128]{1,0:T(8,128)(2,1)S(1)} %collective-permute-done.2.refs_5_) | copy-start | bytes 393220
  18.8 2.9 %copy-start.3 = (bf16[512,128]{1,0:T(8,128)(2,1)}, bf16[512,128]{1,0:T(8,128)(2,1)S(1)}, u32[]{:S(2)}) copy-start(bf16[512,128]{1,0:T(8,128)(2,1)S(1)} %collective-permute-done.1.refs_4_) | copy-start | bytes 393220
  18.8 2.9 %copy-start.4 = (bf16[512,128]{1,0:T(8,128)(2,1)}, bf16[512,128]{1,0:T(8,128)(2,1)S(1)}, u32[]{:S(2)}) copy-start(bf16[512,128]{1,0:T(8,128)(2,1)S(1)} %collective-permute-done.refs_3_) | copy-start | bytes 393220
  21.7 22.5 %collective-permute-start.3 = (bf16[1,256,640]{2,1,0:T(8,128)(2,1)S(1)}, bf16[1,256,640]{2,1,0:T(8,128)(2,1)S(1)}, u32[]{:S(2)}, u32[]{:S(2)}) collective-permute-start(bf16[1,256,640]{2,1,0:T(8,128)(2,1)S(1)} %attend.2), channel_id=1, source_target_pairs={{0,2},{2,0},{1,3},{3,1},{4,6},{6,4},{5,7},{7,5},{8,10},{10,8},{9,1... | collective-permute-start | bytes 983048 | tf_op jit(solution)/shard_map/ppermute | solution.py:398
  23.2 9.8 %collective-permute-start.9 = (bf16[512,128]{1,0:T(8,128)(2,1)S(1)}, bf16[512,128]{1,0:T(8,128)(2,1)S(1)}, u32[]{:S(2)}, u32[]{:S(2)}) collective-permute-start(bf16[512,128]{1,0:T(8,128)(2,1)S(1)} %collective-permute-done.6.refs_2_), channel_id=1, source_target_pairs={{0,12},{4,8},{8,4},{12,0},{1,13},{5,9},{9,5},{13,1},{2,14},{6,10},... | collective-permute-start | bytes 393224 | tf_op jit(solution)/shard_map/ppermute | solution.py:80
  24.7 11.3 %collective-permute-start.8 = (bf16[512,128]{1,0:T(8,128)(2,1)S(1)}, bf16[512,128]{1,0:T(8,128)(2,1)S(1)}, u32[]{:S(2)}, u32[]{:S(2)}) collective-permute-start(bf16[512,128]{1,0:T(8,128)(2,1)S(1)} %collective-permute-done.6.refs_2_), channel_id=1, source_target_pairs={{0,8},{4,12},{8,0},{12,4},{1,9},{5,13},{9,1},{13,5},{2,10},{6,14},... | collective-permute-start | bytes 393224 | tf_op jit(solution)/shard_map/ppermute | solution.py:80
  24.7 5.9 %collective-permute-start.4 = (s32[1,7]{1,0:T(1,128)S(1)}, s32[1,7]{1,0:T(1,128)S(1)}, u32[]{:S(2)}, u32[]{:S(2)}) collective-permute-start(s32[1,7]{1,0:T(1,128)S(1)} %pad_add_fusion.refs_0_), channel_id=1, source_target_pairs={{0,2},{2,0},{1,3},{3,1},{4,6},{6,4},{5,7},{7,5},{8,10},{10,8},{9,1... | collective-permute-start | bytes 92 | tf_op jit(solution)/shard_map/ppermute | solution.py:398
  30.6 7.2 %collective-permute-start.7 = (bf16[512,128]{1,0:T(8,128)(2,1)S(1)}, bf16[512,128]{1,0:T(8,128)(2,1)S(1)}, u32[]{:S(2)}, u32[]{:S(2)}) collective-permute-start(bf16[512,128]{1,0:T(8,128)(2,1)S(1)} %collective-permute-done.6.refs_2_), channel_id=1, source_target_pairs={{0,4},{4,0},{8,12},{12,8},{1,5},{5,1},{9,13},{13,9},{2,6},{6,2},{1... | collective-permute-start | bytes 393224 | tf_op jit(solution)/shard_map/ppermute | solution.py:80
  33.0 11.0 %collective-permute-start.10 = (bf16[256,128]{1,0:T(8,128)(2,1)}, bf16[256,128]{1,0:T(8,128)(2,1)S(1)}, u32[]{:S(2)}, u32[]{:S(2)}) collective-permute-start(bf16[256,128]{1,0:T(8,128)(2,1)} %get-tuple-element.17), channel_id=1, source_target_pairs={{0,4},{4,0},{8,12},{12,8},{1,5},{5,1},{9,13},{13,9},{2,6},{6,2},{1... | collective-permute-start | bytes 196616 | tf_op jit(solution)/shard_map/ppermute | solution.py:80
  36.0 8.0 %collective-permute-start.11 = (bf16[256,128]{1,0:T(8,128)(2,1)}, bf16[256,128]{1,0:T(8,128)(2,1)S(1)}, u32[]{:S(2)}, u32[]{:S(2)}) collective-permute-start(bf16[256,128]{1,0:T(8,128)(2,1)} %get-tuple-element.18), channel_id=1, source_target_pairs={{0,8},{4,12},{8,0},{12,4},{1,9},{5,13},{9,1},{13,5},{2,10},{6,14},... | collective-permute-start | bytes 196616 | tf_op jit(solution)/shard_map/ppermute | solution.py:80
  37.8 6.3 %collective-permute-start.12 = (bf16[256,128]{1,0:T(8,128)(2,1)}, bf16[256,128]{1,0:T(8,128)(2,1)S(1)}, u32[]{:S(2)}, u32[]{:S(2)}) collective-permute-start(bf16[256,128]{1,0:T(8,128)(2,1)} %get-tuple-element.19), channel_id=1, source_target_pairs={{0,12},{4,8},{8,4},{12,0},{1,13},{5,9},{9,5},{13,1},{2,14},{6,10},... | collective-permute-start | bytes 196616 | tf_op jit(solution)/shard_map/ppermute | solution.py:80
